TPU v7x, 32 devices: a whole 2x2x4 slice. The times are simulated.
32 devices in a mesh: row: 4 (over x, core), col: 8 (over z, y).
Axes of the slice: x: 2, y: 2, z: 4, core: 2. Of those that a mesh axis runs over, the one named last changes fastest.
Arguments:
- embeddings: bfloat16 [4096, 512], P(('row', 'col')), may hold values from -6 to 6
- sketch: bfloat16 [4096, 64], P(('row', 'col')), may hold values from -240 to 240
Outputs:
- basis: float32 [4096, 64], P(('row', 'col'))
- first_pass: float32 [4096, 64], P(('row', 'col'))
All inputs are finite; a program needn't handle non-finite values.
Results may differ from a plain program's by a relative error of at most 0.00205.
Values may be sent and summed in bfloat16 or wider, within the bound.
No kernel may reach another device: no remote copies, remote signals or barrier semaphores. Data moves between devices by JAX's collectives and lax.ppermute only.
A program may use at most 64 MiB of HBM per device.

v0:
```python
import jax
import jax.numpy as jnp
from jax import lax
from jax.sharding import PartitionSpec as P


def squares_of(points):
    return jnp.sum(jnp.square(points.astype(jnp.float32)), axis=1)


def kernel_tile(left, right, left_sq, right_sq, gamma):
    cross = lax.dot_general(
        left, right, (((1,), (1,)), ((), ())), preferred_element_type=jnp.float32
    )
    dist = left_sq[:, None] + right_sq[None, :] - 2.0 * cross
    return jnp.exp(-gamma * dist).astype(jnp.bfloat16)


def product_of(left, right):
    return lax.dot_general(
        left,
        right,
        (((0,), (0,)), ((), ())),
        precision=lax.Precision.HIGHEST,
        preferred_element_type=jnp.float32,
    )


def per_device(embeddings, sketch):
    width = embeddings.shape[1]
    gamma = 3.0 / width
    own_points = lax.all_gather(embeddings, "row", axis=0, tiled=True)
    own_sq = squares_of(own_points)
    empty = jnp.zeros((own_points.shape[0], sketch.shape[1]), jnp.float32)
    total = empty
    points = lax.all_gather(embeddings, "col", axis=0, tiled=True)
    tests = lax.all_gather(sketch, "col", axis=0, tiled=True)
    count = points.shape[0]
    size = 512

    def step(carry, block):
        block_points, block_tests = block
        tile = kernel_tile(own_points, block_points, own_sq, squares_of(block_points), gamma)
        return (carry + jnp.dot(tile, block_tests, preferred_element_type=jnp.float32), None)

    stacked = (
        points.reshape(count // size, size, width),
        tests.reshape(count // size, size, tests.shape[1]),
    )
    total, unused = lax.scan(step, total, stacked)
    sketched = lax.psum_scatter(total, "row", scatter_dimension=0, tiled=True)
    core = lax.psum(product_of(sketch.astype(jnp.float32), sketched), ("row", "col"))
    lower = jnp.linalg.cholesky(core)
    first = jax.scipy.linalg.solve_triangular(lower, sketched.T, lower=True).T
    gram_two = lax.psum(product_of(first, first), ("row", "col"))
    lower_two = jnp.linalg.cholesky(gram_two)
    second = jax.scipy.linalg.solve_triangular(lower_two, first.T, lower=True).T
    total_points = sketched.shape[0] * lax.axis_size("row") * lax.axis_size("col")
    scale = jnp.sqrt(jnp.float32(total_points))
    return (second * scale, first * scale)


def solution(mesh):
    placed = (P(("row", "col"), None), P(("row", "col"), None))
    return jax.shard_map(
        per_device,
        mesh=mesh,
        in_specs=placed,
        out_specs=(P(("row", "col"), None), P(("row", "col"), None)),
        check_vma=False,
    )
```

profile of v0, /device:TPU:0, one launch (start us, length us, event | category | flops | bytes accessed | tf_op | source)
XLA Modules:
  0.0 193.4 jit_solution(8559707278417701284)
XLA Ops:
  7.2 0.0 copy-start.3
  7.2 0.0 all-gather.2.cloned.1.call-start
  7.2 0.7 all-gather.2.cloned.1.call-update
  7.9 0.0 reduce-scatter.2.cloned.1.call-start
  8.0 0.0 copy-done.3
  8.0 28.2 %all_gather.11 = bf16[1024,64]{0,1:T(8,128)(2,1)S(1)} all-gather(bf16[128,64]{0,1:T(8,128)(2,1)S(1)} %copy-done.3), channel_id=1, replica_groups=mesh['row'=4,'col'=8] {'col'}, dimensions={0}, use_global_device_ids=true | all-gather | bytes 147456 | tf_op jit(solution)/shard_map/all_gather | solution.py:37
  36.2 0.0 copy-start
  36.2 0.2 copy.4
  36.4 0.7 copy-done
  37.1 7.2 %all_gather.9 = bf16[512,512]{1,0:T(8,128)(2,1)S(1)} all-gather(bf16[128,512]{1,0:T(8,128)(2,1)S(1)} %copy-done), channel_id=1, replica_groups=mesh['row'=4,'col'=8] {'row'}, dimensions={0}, use_global_device_ids=true | all-gather | bytes 655360 | tf_op jit(solution)/shard_map/all_gather | solution.py:32
  44.3 0.2 multiply_reduce_fusion.1
  44.5 9.1 %all-gather.2.cloned.1.call-done = bf16[1024,512]{1,0:T(8,128)(2,1)} async-done(((bf16[128,512]{1,0:T(8,128)(2,1)}), bf16[1024,512]{1,0:T(8,128)(2,1)}) %all-gather.2.cloned.1.call-update) | async-done | bytes 1048592 | tf_op jit(solution)/shard_map/all_gather | solution.py:36
  53.6 6.2 %while.11 = (s32[]{:T(128)}, f32[512,64]{0,1:T(8,128)S(1)}, f32[512]{0:T(512)S(1)}, bf16[2,512,512]{2,1,0:T(8,128)(2,1)}, bf16[512,512]{1,0:T(8,128)(2,1)S(1)}, ...) while((s32[]{:T(128)}, f32[512,64]{0,1:T(8,128)S(1)}, f32[512]{0:T(512)S(1)}, ...), condition=%wide.region_3.4_spmd.clone, body=%wide.region_1.3_spmd.clone.sunk | while | flops 304152064 | bytes 1973347 | solution.py:50
  53.6 1.2 multiply_reduce_fusion.3
  54.8 1.8 fusion.47
  56.6 1.2 multiply_reduce_fusion.3
  57.9 1.8 fusion.47
  59.7 0.0 copy-start.2
  59.7 0.6 copy-done.2
  60.4 0.0 reduce-scatter.2.cloned.1.call-update
  60.4 18.5 %reduce-scatter.2.cloned.1.call-done = f32[128,64]{0,1:T(8,128)} async-done(((f32[512,64]{0,1:T(8,128)}), f32[128,64]{0,1:T(8,128)}) %reduce-scatter.2.cloned.1.call-update) | async-done | bytes 32784 | tf_op jit(solution)/shard_map/reduce_scatter | solution.py:51
  78.9 0.9 convolution_bitcast_fusion
  79.8 39.4 %psum.14 = f32[64,64]{0,1:T(8,128)S(1)} all-reduce(f32[64,64]{0,1:T(8,128)S(1)} %convolution_bitcast_fusion), channel_id=1, replica_groups=mesh['row'=4,'col'=8] {'row','col'}, use_global_device_ids=true, to_apply=%region_5.6 | all-reduce | flops 4096 | bytes 32768 | tf_op jit(solution)/shard_map/psum | solution.py:52
  119.3 0.1 copy.5
  119.3 5.8 %cholesky.44 = f32[64,64]{1,0:T(8,128)S(1)} custom-call(f32[64,64]{1,0:T(8,128)S(1)} %fusion.30), custom_call_target="Cholesky" | custom-call | tf_op jit(solution)/shard_map/jit(cholesky)/cholesky | solution.py:53
  125.2 0.6 compare_reduce_fusion.1
  125.9 0.0 copy-start.1
  125.9 0.7 fusion.23
  126.5 4.9 %custom-call.7 = f32[1,64,64]{1,2,0:T(8,128)S(1)} custom-call(f32[1,64,64]{2,1,0:T(8,128)S(1)} %fusion.23), custom_call_target="InvertDiagBlocksLowerTriangular" | custom-call | tf_op jit(solution)/shard_map/jit(_solve_triangular)/triangular_solve | solution.py:54
  131.4 0.0 copy-done.1
  131.5 0.2 fusion.27
  131.7 0.2 fusion.33
  131.9 0.6 multiply_bitcast_fusion
  132.5 41.0 %psum.15 = f32[64,64]{0,1:T(8,128)S(1)} all-reduce(f32[64,64]{0,1:T(8,128)S(1)} %fusion.33), channel_id=1, replica_groups=mesh['row'=4,'col'=8] {'row','col'}, use_global_device_ids=true, to_apply=%region_8.11 | all-reduce | flops 4096 | bytes 32768 | tf_op jit(solution)/shard_map/psum | solution.py:55
  173.5 0.1 copy.7
  173.6 5.8 %cholesky.55 = f32[64,64]{1,0:T(8,128)S(1)} custom-call(f32[64,64]{1,0:T(8,128)S(1)} %fusion.26), custom_call_target="Cholesky" | custom-call | tf_op jit(solution)/shard_map/jit(cholesky)/cholesky | solution.py:56
  179.5 0.6 compare_reduce_fusion
  180.2 0.7 fusion.24
  180.8 4.9 %custom-call.8 = f32[1,64,64]{1,2,0:T(8,128)S(1)} custom-call(f32[1,64,64]{2,1,0:T(8,128)S(1)} %fusion.24), custom_call_target="InvertDiagBlocksLowerTriangular" | custom-call | tf_op jit(solution)/shard_map/jit(_solve_triangular)/triangular_solve | solution.py:57
  185.7 0.9 fusion.22
  (5 shorter events, 0.1 us)
Async XLA Ops:
  7.2 0.8 copy-start.3
  7.2 46.4 %all-gather.2.cloned.1.call-start = ((), (), s32[]{:S(2)}) async-start(), calls=%async_computation.1 | async-start | bytes 1179648 | tf_op jit(solution)/shard_map/all_gather | solution.py:36
  7.9 71.0 %reduce-scatter.2.cloned.1.call-start = ((), (), s32[]{:S(2)}) async-start(), calls=%async_computation.2 | async-start | bytes 163840 | tf_op jit(solution)/shard_map/reduce_scatter | solution.py:51
  36.2 0.9 copy-start
  59.7 0.6 copy-start.2
  125.9 5.6 %copy-start.1 = (f32[128,64]{0,1:T(8,128)S(1)}, f32[128,64]{0,1:T(8,128)}, u32[]{:S(2)}) copy-start(f32[128,64]{0,1:T(8,128)} %reduce-scatter.2.cloned.1.call-done) | copy-start | bytes 98308
Sparse Core Ops, SparseCore 0:
  10.1 43.4 all-gather.1
  60.5 18.3 reduce-scatter.1
where the time goes:
time: 194 us; the launch traced here: 193 us
  blocking collectives  116 us (60%)
  waiting for transfers between devices  28.3 us (15%)
  other arithmetic  27.4 us (14%)
  between operations  14.2 us (7%)
  matrix products  5.88 us (3%)
    psum x1, blocking collectives, per_device(): gram_two = lax.psum(product_of(first, first), ('row', 'col'))  41 us
    psum x1, blocking collectives, per_device(): lax.psum(product_of(sketch.astype(jnp.float32), sketched), ('row', 'col'))  39.4 us
    all_gather x1, blocking collectives, per_device(): tests = lax.all_gather(sketch, 'col', axis=0, tiled=True)  28.2 us
    reduce_scatter x1, waiting for transfers between devices, per_device(): sketched = lax.psum_scatter(total, 'row', scatter_dimension=0, tiled=True)  18.5 us
    all_gather x1, waiting for transfers between devices, per_device(): points = lax.all_gather(embeddings, 'col', axis=0, tiled=True)  9.11 us
    all_gather x1, blocking collectives, per_device(): own_points = lax.all_gather(embeddings, 'row', axis=0, tiled=True)  7.18 us
    another operation x3, other arithmetic, per_device(): lower_two = jnp.linalg.cholesky(gram_two)  6.52 us
    another operation x3, other arithmetic, per_device(): lower = jnp.linalg.cholesky(core)  6.52 us
  transfers between devices with their start and end apart: 2, of which 2 were waited for; matrix products, arithmetic and copies ran while one was open for 0% of the time, Pallas kernels for 0%

commit v1 on v0

--- a/solution.py
+++ b/solution.py
@@ -52,7 +52,9 @@
     core = lax.psum(product_of(sketch.astype(jnp.float32), sketched), ("row", "col"))
     lower = jnp.linalg.cholesky(core)
     first = jax.scipy.linalg.solve_triangular(lower, sketched.T, lower=True).T
-    gram_two = lax.psum(product_of(first, first), ("row", "col"))
+    part = product_of(first, first)
+    parts = lax.all_gather(part, ("row", "col"))
+    gram_two = jnp.sum(parts, axis=0)
     lower_two = jnp.linalg.cholesky(gram_two)
     second = jax.scipy.linalg.solve_triangular(lower_two, first.T, lower=True).T
     total_points = sketched.shape[0] * lax.axis_size("row") * lax.axis_size("col")

time: 194 us -> 226 us (1.16)
  blocking collectives: 116 us -> 148 us
    all_gather x0 -> x1, blocking collectives: none -> 73.1 us  [per_device(): parts = lax.all_gather(part, ('row', 'col'))]
    psum x1 -> x0, blocking collectives: 41 us -> none  [per_device(): gram_two = lax.psum(product_of(first, first), ('row', 'col'))]
where the time goes in v1:
time: 226 us
  blocking collectives  148 us (65%)
  waiting for transfers between devices  28.3 us (13%)
  other arithmetic  27.5 us (12%)
  between operations  14.2 us (6%)
  matrix products  5.88 us (3%)
    all_gather x1, blocking collectives, per_device(): parts = lax.all_gather(part, ('row', 'col'))  73.1 us
    psum x1, blocking collectives, per_device(): lax.psum(product_of(sketch.astype(jnp.float32), sketched), ('row', 'col'))  39.4 us
    all_gather x1, blocking collectives, per_device(): tests = lax.all_gather(sketch, 'col', axis=0, tiled=True)  28.2 us
    reduce_scatter x1, waiting for transfers between devices, per_device(): sketched = lax.psum_scatter(total, 'row', scatter_dimension=0, tiled=True)  18.5 us
    all_gather x1, waiting for transfers between devices, per_device(): points = lax.all_gather(embeddings, 'col', axis=0, tiled=True)  9.11 us
    all_gather x1, blocking collectives, per_device(): own_points = lax.all_gather(embeddings, 'row', axis=0, tiled=True)  7.18 us
    another operation x3, other arithmetic, per_device(): lower_two = jnp.linalg.cholesky(gram_two)  6.52 us
    another operation x3, other arithmetic, per_device(): lower = jnp.linalg.cholesky(core)  6.52 us
  transfers between devices with their start and end apart: 2, of which 2 were waited for; matrix products, arithmetic and copies ran while one was open for 0% of the time, Pallas kernels for 0%

profile of v1, /device:TPU:0, one launch (start us, length us, event | category | flops | bytes accessed | tf_op | source)
XLA Modules:
  0.0 225.6 jit_solution(6368206625257600249)
XLA Ops:
  7.2 0.0 copy-start.3
  7.2 0.0 all-gather.3.cloned.1.call-start
  7.2 0.7 all-gather.3.cloned.1.call-update
  7.9 0.0 reduce-scatter.2.cloned.1.call-start
  8.0 0.0 copy-done.3
  8.0 28.2 %all_gather.17 = bf16[1024,64]{0,1:T(8,128)(2,1)S(1)} all-gather(bf16[128,64]{0,1:T(8,128)(2,1)S(1)} %copy-done.3), channel_id=1, replica_groups=mesh['row'=4,'col'=8] {'col'}, dimensions={0}, use_global_device_ids=true | all-gather | bytes 147456 | tf_op jit(solution)/shard_map/all_gather | solution.py:37
  36.2 0.0 copy-start
  36.2 0.2 copy.7
  36.4 0.7 copy-done
  37.1 7.2 %all_gather.15 = bf16[512,512]{1,0:T(8,128)(2,1)S(1)} all-gather(bf16[128,512]{1,0:T(8,128)(2,1)S(1)} %copy-done), channel_id=1, replica_groups=mesh['row'=4,'col'=8] {'row'}, dimensions={0}, use_global_device_ids=true | all-gather | bytes 655360 | tf_op jit(solution)/shard_map/all_gather | solution.py:32
  44.3 0.2 multiply_reduce_fusion.1
  44.5 9.1 %all-gather.3.cloned.1.call-done = bf16[1024,512]{1,0:T(8,128)(2,1)} async-done(((bf16[128,512]{1,0:T(8,128)(2,1)}), bf16[1024,512]{1,0:T(8,128)(2,1)}) %all-gather.3.cloned.1.call-update) | async-done | bytes 1048592 | tf_op jit(solution)/shard_map/all_gather | solution.py:36
  53.6 6.2 %while.11 = (s32[]{:T(128)}, f32[512,64]{0,1:T(8,128)S(1)}, f32[512]{0:T(512)S(1)}, bf16[2,512,512]{2,1,0:T(8,128)(2,1)}, bf16[512,512]{1,0:T(8,128)(2,1)S(1)}, ...) while((s32[]{:T(128)}, f32[512,64]{0,1:T(8,128)S(1)}, f32[512]{0:T(512)S(1)}, ...), condition=%wide.region_3.4_spmd.clone, body=%wide.region_1.3_spmd.clone.sunk | while | flops 304152064 | bytes 1973347 | solution.py:50
  53.6 1.2 multiply_reduce_fusion.3
  54.8 1.8 fusion.47
  56.6 1.2 multiply_reduce_fusion.3
  57.9 1.8 fusion.47
  59.7 0.0 copy-start.2
  59.7 0.6 copy-done.2
  60.4 0.0 reduce-scatter.2.cloned.1.call-update
  60.4 18.5 %reduce-scatter.2.cloned.1.call-done = f32[128,64]{0,1:T(8,128)} async-done(((f32[512,64]{0,1:T(8,128)}), f32[128,64]{0,1:T(8,128)}) %reduce-scatter.2.cloned.1.call-update) | async-done | bytes 32784 | tf_op jit(solution)/shard_map/reduce_scatter | solution.py:51
  78.9 0.9 convolution_bitcast_fusion
  79.8 39.4 %psum.7 = f32[64,64]{0,1:T(8,128)S(1)} all-reduce(f32[64,64]{0,1:T(8,128)S(1)} %convolution_bitcast_fusion), channel_id=1, replica_groups=mesh['row'=4,'col'=8] {'row','col'}, use_global_device_ids=true, to_apply=%region_5.6 | all-reduce | flops 4096 | bytes 32768 | tf_op jit(solution)/shard_map/psum | solution.py:52
  119.3 0.1 copy.8
  119.3 5.8 %cholesky.44 = f32[64,64]{1,0:T(8,128)S(1)} custom-call(f32[64,64]{1,0:T(8,128)S(1)} %fusion.30), custom_call_target="Cholesky" | custom-call | tf_op jit(solution)/shard_map/jit(cholesky)/cholesky | solution.py:53
  125.2 0.6 compare_reduce_fusion.1
  125.9 0.0 copy-start.1
  125.9 0.7 fusion.23
  126.5 4.9 %custom-call.7 = f32[1,64,64]{1,2,0:T(8,128)S(1)} custom-call(f32[1,64,64]{2,1,0:T(8,128)S(1)} %fusion.23), custom_call_target="InvertDiagBlocksLowerTriangular" | custom-call | tf_op jit(solution)/shard_map/jit(_solve_triangular)/triangular_solve | solution.py:54
  131.4 0.0 copy-done.1
  131.5 0.2 fusion.27
  131.7 0.2 fusion.33
  131.9 0.6 multiply_bitcast_fusion
  132.5 73.1 %all-gather = f32[2048,64]{1,0:T(8,128)S(1)} all-gather(f32[64,64]{1,0:T(8,128)S(1)} %fusion.33), channel_id=2, replica_groups=mesh['row'=4,'col'=8] {'row','col'}, dimensions={0}, use_global_device_ids=true | all-gather | bytes 540672 | tf_op jit(solution)/shard_map/all_gather | solution.py:56
  205.6 0.1 reduce_sum.28
  205.7 0.1 copy.9
  205.8 5.8 %cholesky.55 = f32[64,64]{1,0:T(8,128)S(1)} custom-call(f32[64,64]{1,0:T(8,128)S(1)} %fusion.26), custom_call_target="Cholesky" | custom-call | tf_op jit(solution)/shard_map/jit(cholesky)/cholesky | solution.py:58
  211.6 0.6 compare_reduce_fusion
  212.3 0.7 fusion.24
  212.9 4.9 %custom-call.8 = f32[1,64,64]{1,2,0:T(8,128)S(1)} custom-call(f32[1,64,64]{2,1,0:T(8,128)S(1)} %fusion.24), custom_call_target="InvertDiagBlocksLowerTriangular" | custom-call | tf_op jit(solution)/shard_map/jit(_solve_triangular)/triangular_solve | solution.py:59
  217.8 0.9 fusion.22
  (5 shorter events, 0.1 us)
Async XLA Ops:
  7.2 0.8 copy-start.3
  7.2 46.4 %all-gather.3.cloned.1.call-start = ((), (), s32[]{:S(2)}) async-start(), calls=%async_computation.1 | async-start | bytes 1179648 | tf_op jit(solution)/shard_map/all_gather | solution.py:36
  7.9 71.0 %reduce-scatter.2.cloned.1.call-start = ((), (), s32[]{:S(2)}) async-start(), calls=%async_computation.2 | async-start | bytes 163840 | tf_op jit(solution)/shard_map/reduce_scatter | solution.py:51
  36.2 0.9 copy-start
  59.7 0.6 copy-start.2
  125.9 5.6 %copy-start.1 = (f32[128,64]{0,1:T(8,128)S(1)}, f32[128,64]{0,1:T(8,128)}, u32[]{:S(2)}) copy-start(f32[128,64]{0,1:T(8,128)} %reduce-scatter.2.cloned.1.call-done) | copy-start | bytes 98308
Sparse Core Ops, SparseCore 0:
  10.1 43.4 all-gather.2
  60.5 18.3 reduce-scatter.1
